TPU v7x, 128 devices: a whole 4x4x4 slice. The times are simulated.
128 devices in a mesh: past: 8 (over y, z_lo), second: 16 (over x, z_hi, core).
Axes of the slice: x: 4, y: 4, z: 4 (z_hi: 2, z_lo: 2; z = z_hi * 2 + z_lo), core: 2. Of those that a mesh axis runs over, the one named last changes fastest.
Arguments:
- resident: bfloat16 [24576, 24576], P('past', 'second'), may hold values from -6 to 6
- memory: bfloat16 [2, 384, 24576], P(None, None, 'past'), may hold values from -0.0390625 to 0.0390625
- previous: bfloat16 [2, 384, 24576], P(None, None, 'second'), may hold values from -6 to 6
- inverse_part: float32 [2, 384, 384], replicated, may hold values from -0.3125 to 0.3125
- pair_coupling: float32 [32, 32], replicated, may hold values from 0.000318944 to 0.00318944
Outputs:
- fronts: bfloat16 [2, 384, 24576], P(None, None, 'second')
All inputs are finite; a program needn't handle non-finite values.
Results may differ from a plain program's by a relative error of at most 0.017.
Values may be sent and summed in bfloat16 or wider, within the bound.
No kernel may reach another device: no remote copies, remote signals or barrier semaphores. Data moves between devices by JAX's collectives and lax.ppermute only.
A program may use at most 128 MiB of HBM per device.

v0:
```python
import jax
import jax.numpy as jnp
from jax import lax
from jax.sharding import PartitionSpec as P

step_size = 0.5


def orbital_flip(block, orbitals):
    row_count, col_count = block.shape
    blocks = block.reshape(row_count // orbitals, orbitals, col_count // orbitals, orbitals)
    return blocks.transpose(0, 3, 2, 1).reshape(row_count, col_count)


def solve_front(summed, prior, inverse_block):
    source = prior.astype(jnp.float32) - step_size * summed
    solved = source + jnp.dot(
        inverse_block, source, precision=lax.Precision.HIGHEST, preferred_element_type=jnp.float32
    )
    return solved.astype(jnp.bfloat16)


def self_energy(front, pair_coupling):
    orbitals = pair_coupling.shape[0]
    row_count, col_count = front.shape
    values = front.astype(jnp.float32)
    mirror = orbital_flip(values, orbitals)
    blocks = (values * values * mirror).reshape(
        row_count // orbitals, orbitals, col_count // orbitals, orbitals
    )
    return (
        (blocks * pair_coupling[None, :, None, :])
        .reshape(row_count, col_count)
        .astype(jnp.bfloat16)
    )


def per_device(resident, memory, previous, inverse_part, pair_coupling):

    def advance(memory_row, front_index):
        partial_value = jnp.dot(memory_row, resident, preferred_element_type=jnp.float32)
        summed = lax.psum(partial_value.astype(jnp.bfloat16), "past").astype(jnp.float32)
        prior_cols = previous[front_index]
        return solve_front(summed, prior_cols, inverse_part[front_index])

    front_one = advance(memory[0], 0)
    energy_one = self_energy(front_one, pair_coupling)
    span_cols = memory.shape[2]
    whole_row = lax.all_gather(energy_one, "second", axis=1, tiled=True)
    gathered = lax.dynamic_slice_in_dim(whole_row, lax.axis_index("past") * span_cols, span_cols, 1)
    orbitals = pair_coupling.shape[0]
    memory_next = (
        memory[1].astype(jnp.float32) + orbital_flip(gathered, orbitals).astype(jnp.float32)
    ).astype(jnp.bfloat16)
    front_two = advance(memory_next, 1)
    return jnp.stack([front_one, front_two])


def solution(mesh):
    in_specs = (P("past", "second"), P(None, None, "past"), P(None, None, "second"), P(), P())
    out_specs = P(None, None, "second")
    return jax.shard_map(
        per_device, mesh=mesh, in_specs=in_specs, out_specs=out_specs, check_vma=False
    )
```

profile of v0, /device:TPU:0, one launch (start us, length us, event | category | flops | bytes accessed | tf_op | source)
XLA Modules:
  0.0 406.2 jit_solution(5935509110012505917)
XLA Ops:
  6.5 0.0 copy-start
  6.5 0.0 all-reduce.3.cloned.1.call-start
  6.5 9.2 %convolution_convert_fusion.1 = bf16[384,1536]{1,0:T(8,128)(2,1)} fusion(bf16[3072,1536]{1,0:T(8,128)(2,1)} %param.5, bf16[2,384,3072]{2,1,0:T(8,128)(2,1)} %param.6), kind=kOutput, calls=%fused_computation.9 | convolution fusion | flops 3624468480 | bytes 12976128 | tf_op jit(solution)/shard_map/dot_general | solution.py:41
  15.8 0.0 all-reduce.3.cloned.1.call-update
  15.8 0.0 all-gather.2.cloned.1.call-start
  15.8 0.0 copy-done
  15.9 4.4 %mul.29 = f32[12,32,48,32]{3,2,1,0:T(8,128)} broadcast(f32[32,32]{1,0:T(8,128)S(1)} %copy-done), dimensions={1,3} | broadcast | bytes 2363392 | tf_op jit(solution)/shard_map/mul | solution.py:32
  20.3 6.7 %mul.30 = f32[384,1536]{1,0:T(8,128)S(1)} reshape(f32[12,32,48,32]{3,2,1,0:T(8,128)} %mul.29) | data formatting | bytes 4718592 | tf_op jit(solution)/shard_map/mul | solution.py:32
  27.0 70.5 %all-reduce.3.cloned.1.call-done = bf16[384,1536]{1,0:T(8,128)(2,1)} async-done(((bf16[384,1536]{1,0:T(8,128)(2,1)}), bf16[384,1536]{1,0:T(8,128)(2,1)}) %all-reduce.3.cloned.1.call-update) | async-done | bytes 1179664 | tf_op jit(solution)/shard_map/psum | solution.py:42
  97.5 6.8 %fusion.3 = bf16[384,1536]{1,0:T(8,128)(2,1)S(1)} fusion(bf16[384,1536]{1,0:T(8,128)(2,1)} %all-reduce.3.cloned.1.call-done, bf16[2,384,1536]{2,1,0:T(8,128)(2,1)} %param.7, f32[2,384,384]{2,1,0:T(8,128)} %param.8), kind=kOutput, calls=%fused_computation.6 | convolution fusion | flops 2723807232 | bytes 6488064 | tf_op jit(solution)/shard_map/dot_general | solution.py:17
  104.3 4.9 %reshape.22 = f32[12,32,48,32]{3,2,1,0:T(8,128)} reshape(bf16[384,1536]{1,0:T(8,128)(2,1)S(1)} %fusion.3) | data formatting | bytes 3538944 | tf_op jit(solution)/shard_map/reshape | solution.py:11
  109.2 10.8 %copy.11 = f32[12,32,48,32]{3,2,1,0:T(8,128)} copy(f32[12,32,48,32]{1,2,3,0:T(8,128)} %bitcast.55) | data formatting | bytes 4718592 | tf_op jit(solution)/shard_map/transpose | solution.py:12
  120.0 7.7 %reshape.23 = f32[384,1536]{1,0:T(8,128)} reshape(f32[12,32,48,32]{3,2,1,0:T(8,128)} %copy.11) | data formatting | bytes 4718592 | tf_op jit(solution)/shard_map/reshape | solution.py:12
  127.8 3.3 multiply_convert_fusion
  131.1 0.0 all-gather.2.cloned.1.call-update
  131.1 0.2 all-reduce.5.cloned.1.call-start
  131.3 119.3 %all-gather.2.cloned.1.call-done = bf16[384,24576]{1,0:T(8,128)(2,1)} async-done(((bf16[384,1536]{1,0:T(8,128)(2,1)}), bf16[384,24576]{1,0:T(8,128)(2,1)}) %all-gather.2.cloned.1.call-update) | async-done | bytes 18874384 | tf_op jit(solution)/shard_map/all_gather | solution.py:49
  250.6 4.4 %dynamic-slice_convert_fusion = f32[384,3072]{1,0:T(8,128)} fusion(bf16[384,24576]{1,0:T(8,128)(2,1)} %all-gather.2.cloned.1.call-done, s32[]{:T(128)S(6)} %select_n.3), kind=kLoop, calls=%fused_computation.18 | loop fusion | flops 1179648 | bytes 7077892 | tf_op jit(solution)/shard_map/convert_element_type | solution.py:53
  255.0 12.3 %reshape.28 = f32[12,32,96,32]{3,2,1,0:T(8,128)} reshape(f32[384,3072]{1,0:T(8,128)} %dynamic-slice_convert_fusion) | data formatting | bytes 9437184 | tf_op jit(solution)/shard_map/convert_element_type | solution.py:53
  267.3 22.5 %copy.12 = f32[12,32,96,32]{3,2,1,0:T(8,128)} copy(f32[12,32,96,32]{1,2,3,0:T(8,128)} %bitcast.54) | data formatting | bytes 9437184 | tf_op jit(solution)/shard_map/convert_element_type | solution.py:53
  289.7 14.6 %reshape.27 = f32[384,3072]{1,0:T(8,128)} reshape(f32[12,32,96,32]{3,2,1,0:T(8,128)} %copy.12) | data formatting | bytes 9437184 | tf_op jit(solution)/shard_map/convert_element_type | solution.py:53
  304.3 0.0 copy-start.1
  304.3 10.7 %convolution_convert_fusion = bf16[384,1536]{1,0:T(8,128)(2,1)} fusion(bf16[3072,1536]{1,0:T(8,128)(2,1)} %param.5, f32[384,3072]{1,0:T(8,128)} %reshape.27, bf16[2,384,3072]{2,1,0:T(8,128)(2,1)} %param.6), kind=kOutput, calls=%fused_computation.8 | convolution fusion | flops 3628007424 | bytes 17694720 | tf_op jit(solution)/shard_map/dot_general | solution.py:41
  315.0 0.0 all-reduce.5.cloned.1.call-update
  315.1 77.0 %all-reduce.5.cloned.1.call-done = bf16[384,1536]{1,0:T(8,128)(2,1)} async-done(((bf16[384,1536]{1,0:T(8,128)(2,1)}), bf16[384,1536]{1,0:T(8,128)(2,1)}) %all-reduce.5.cloned.1.call-update) | async-done | bytes 1179664 | tf_op jit(solution)/shard_map/psum | solution.py:42
  392.0 0.0 copy-done.1
  392.0 6.1 %fusion.5 = bf16[1,384,1536]{2,1,0:T(8,128)(2,1)S(1)} fusion(bf16[384,1536]{1,0:T(8,128)(2,1)} %all-reduce.5.cloned.1.call-done, bf16[2,384,1536]{2,1,0:T(8,128)(2,1)S(1)} %copy-done.1, f32[2,384,384]{2,1,0:T(8,128)} %param.8), kind=kOutput, calls=%fused_computation.10 | convolution fusion | flops 2723807232 | bytes 6488064 | tf_op jit(solution)/shard_map/dot_general | solution.py:17
  398.1 1.6 pad_maximum_fusion
Async XLA Ops:
  6.5 9.3 %copy-start = (f32[32,32]{1,0:T(8,128)S(1)}, f32[32,32]{1,0:T(8,128)}, u32[]{:S(2)}) copy-start(f32[32,32]{1,0:T(8,128)} %param.9) | copy-start | bytes 12292
  6.5 91.0 %all-reduce.3.cloned.1.call-start = ((), (), s32[]{:S(2)}) async-start(), calls=%async_computation | async-start | bytes 2359296 | tf_op jit(solution)/shard_map/psum | solution.py:42
  15.8 234.8 %all-gather.2.cloned.1.call-start = ((), (), s32[]{:S(2)}) async-start(), calls=%async_computation.1 | async-start | bytes 20054016 | tf_op jit(solution)/shard_map/all_gather | solution.py:49
  131.1 260.9 %all-reduce.5.cloned.1.call-start = ((), (), s32[]{:S(2)}) async-start(), calls=%async_computation.2 | async-start | bytes 2359296 | tf_op jit(solution)/shard_map/psum | solution.py:42
  304.3 87.7 %copy-start.1 = (bf16[2,384,1536]{2,1,0:T(8,128)(2,1)S(1)}, bf16[2,384,1536]{2,1,0:T(8,128)(2,1)}, u32[]{:S(2)}) copy-start(bf16[2,384,1536]{2,1,0:T(8,128)(2,1)} %param.7) | copy-start | bytes 7077892
Sparse Core Ops, SparseCore 0:
  15.9 81.5 all-reduce.2
  131.2 119.3 all-gather.1
  315.2 76.7 all-reduce.4
where the time goes:
time: 407 us; the launch traced here: 406 us
  waiting for transfers between devices  267 us (66%)
  local copies, waits for them, and re-layouts  83.9 us (21%)
  matrix products  32.8 us (8%)
  between operations  13.1 us (3%)
  other arithmetic  9.31 us (2%)
    psum x2, waiting for transfers between devices, advance(): lax.psum(partial_value.astype(jnp.bfloat16), 'past').astype(jnp.float32)  147 us
    all_gather x1, waiting for transfers between devices, per_device(): whole_row = lax.all_gather(energy_one, 'second', axis=1, tiled=True)  119 us
    convert_element_type x3, local copies, waits for them, and re-layouts, per_device(): orbital_flip(gathered, orbitals).astype(jnp.float32)  49.3 us
    dot_general x2, matrix products, advance(): jnp.dot(memory_row, resident, preferred_element_type=jnp.float32)  19.9 us
    dot_general x2, matrix products, solve_front(): jnp.dot(inverse_block, source, precision=lax.Precision.HIGHEST, preferred...  12.9 us
    mul x2, local copies, waits for them, and re-layouts, self_energy(): blocks * pair_coupling[None, :, None, :]  11.2 us
    transpose x1, local copies, waits for them, and re-layouts, orbital_flip(): return blocks.transpose(0, 3, 2, 1).reshape(row_count, col_count)  10.8 us
  transfers between devices with their start and end apart: 3, of which 3 were waited for; matrix products, arithmetic and copies ran while one was open for 3% of the time, Pallas kernels for 0%

commit v1 on v0

--- a/solution.py
+++ b/solution.py
@@ -4,6 +4,11 @@
 from jax.sharding import PartitionSpec as P
 
 step_size = 0.5
+
+
+def move_sizes_now(raw, bus_axis):
+    arr_out = jax.lax.all_gather(raw, axis_name=bus_axis).sum(axis=0)
+    return arr_out
 
 
 def orbital_flip(block, orbitals):
@@ -39,7 +44,7 @@
 
     def advance(memory_row, front_index):
         partial_value = jnp.dot(memory_row, resident, preferred_element_type=jnp.float32)
-        summed = lax.psum(partial_value.astype(jnp.bfloat16), "past").astype(jnp.float32)
+        summed = move_sizes_now(partial_value.astype(jnp.bfloat16), "past").astype(jnp.float32)
         prior_cols = previous[front_index]
         return solve_front(summed, prior_cols, inverse_part[front_index])
 

time: 407 us -> 658 us (1.62)
  waiting for transfers between devices: 267 us -> 483 us
  local copies, waits for them, and re-layouts: 83.9 us -> 104 us
  other arithmetic: 9.31 us -> 18.9 us
    all_gather x0 -> x2, waiting for transfers between devices: none -> 360 us  [move_sizes_now(): arr_out = jax.lax.all_gather(raw, axis_name=bus_axis).sum(axis=0)]
    psum x2 -> x0, waiting for transfers between devices: 147 us -> none  [advance(): lax.psum(partial_value.astype(jnp.bfloat16), 'past').astype(jnp.float32)]
    reshape x1 -> x2, local copies, waits for them, and re-layouts: 7.74 us -> 22.1 us  [orbital_flip(): return blocks.transpose(0, 3, 2, 1).reshape(row_count, col_count)]
    reduce_sum x0 -> x2, other arithmetic: none -> 11.4 us  [move_sizes_now(): arr_out = jax.lax.all_gather(raw, axis_name=bus_axis).sum(axis=0)]
    transpose x1 -> x0, local copies, waits for them, and re-layouts: 10.8 us -> none  [orbital_flip(): return blocks.transpose(0, 3, 2, 1).reshape(row_count, col_count)]
    convert_element_type x3 -> x4, local copies, waits for them, and re-layouts: 49.3 us -> 55.4 us  [per_device(): orbital_flip(gathered, orbitals).astype(jnp.float32)]
    mul x2 -> x3, local copies, waits for them, and re-layouts: 11.2 us -> 13.3 us  [self_energy(): blocks * pair_coupling[None, :, None, :]]
  transfers between devices with their start and end apart: 3 -> 3, of which waited for: 3 -> 3; matrix products, arithmetic and copies ran while one was open for 3% -> 2% of each run, Pallas kernels for 0% -> 0%
where the time goes in v1:
time: 658 us; the launch traced here: 652 us
  waiting for transfers between devices  483 us (73%)
  local copies, waits for them, and re-layouts  104 us (16%)
  matrix products  32.6 us (5%)
  other arithmetic  18.9 us (3%)
  between operations  13.2 us (2%)
    all_gather x2, waiting for transfers between devices, move_sizes_now(): arr_out = jax.lax.all_gather(raw, axis_name=bus_axis).sum(axis=0)  360 us
    all_gather x1, waiting for transfers between devices, per_device(): whole_row = lax.all_gather(energy_one, 'second', axis=1, tiled=True)  123 us
    convert_element_type x4, local copies, waits for them, and re-layouts, per_device(): orbital_flip(gathered, orbitals).astype(jnp.float32)  55.4 us
    reshape x2, local copies, waits for them, and re-layouts, orbital_flip(): return blocks.transpose(0, 3, 2, 1).reshape(row_count, col_count)  22.1 us
    dot_general x2, matrix products, advance(): jnp.dot(memory_row, resident, preferred_element_type=jnp.float32)  20 us
    mul x3, local copies, waits for them, and re-layouts, self_energy(): blocks * pair_coupling[None, :, None, :]  13.3 us
  transfers between devices with their start and end apart: 3, of which 3 were waited for; matrix products, arithmetic and copies ran while one was open for 2% of the time, Pallas kernels for 0%

profile of v1, /device:TPU:0, one launch (start us, length us, event | category | flops | bytes accessed | tf_op | source)
XLA Modules:
  0.0 652.0 jit_solution(3939210395595429389)
XLA Ops:
  6.5 0.0 all-gather.8.cloned.1.call-start
  6.5 0.0 copy-start.1
  6.5 9.4 %convolution_convert_fusion.1 = bf16[384,1536]{1,0:T(8,128)(2,1)} fusion(bf16[3072,1536]{1,0:T(8,128)(2,1)} %param.5, bf16[2,384,3072]{2,1,0:T(8,128)(2,1)} %param.6), kind=kOutput, calls=%fused_computation.13 | convolution fusion | flops 3624468480 | bytes 12976128 | tf_op jit(solution)/shard_map/dot_general | solution.py:46
  15.9 0.0 all-gather.8.cloned.1.call-update
  15.9 0.0 all-gather.6.cloned.1.call-start
  16.0 0.0 copy-done.1
  16.0 1.2 fusion.31
  17.2 0.0 copy-start.2
  17.2 0.7 copy.34
  17.9 0.0 copy-done.2
  17.9 4.5 mul.50
  22.4 6.9 %mul.51 = f32[384,1536]{1,0:T(8,128)S(1)} reshape(f32[12,32,48,32]{3,2,1,0:T(8,128)} %mul.50) | data formatting | bytes 4718592 | tf_op jit(solution)/shard_map/mul | solution.py:37
  29.3 2.0 copy.27
  31.3 175.4 %all-gather.8.cloned.1.call-done = bf16[3072,1536]{1,0:T(8,128)(2,1)} async-done(((bf16[384,1536]{1,0:T(8,128)(2,1)}), bf16[3072,1536]{1,0:T(8,128)(2,1)}) %all-gather.8.cloned.1.call-update) | async-done | bytes 9437200 | tf_op jit(solution)/shard_map/all_gather | solution.py:10
  206.6 5.7 reduce_sum.24
  212.3 0.7 copy.22
  213.1 5.7 fusion.3
  218.8 0.6 copy.24
  219.5 4.9 reshape.50
  224.3 13.9 %copy.32 = f32[12,32,48,32]{1,0,3,2:T(8,128)} copy(f32[12,32,48,32]{1,2,3,0:T(8,128)} %bitcast.73) | data formatting | bytes 4718592 | tf_op jit(solution)/shard_map/reshape | solution.py:17
  238.2 8.2 %reshape.59 = f32[384,1536]{0,1:T(8,128)S(1)} reshape(f32[12,32,48,32]{1,0,3,2:T(8,128)} %copy.32) | data formatting | bytes 4718592 | tf_op jit(solution)/shard_map/reshape | solution.py:17
  246.4 3.1 multiply_convert_fusion
  249.5 0.0 all-gather.6.cloned.1.call-update
  249.5 0.0 all-gather.10.cloned.1.call-start
  249.5 123.1 %all-gather.6.cloned.1.call-done = bf16[384,24576]{0,1:T(8,128)(2,1)} async-done(((bf16[384,1536]{0,1:T(8,128)(2,1)}), bf16[384,24576]{0,1:T(8,128)(2,1)}) %all-gather.6.cloned.1.call-update) | async-done | bytes 18874384 | tf_op jit(solution)/shard_map/all_gather | solution.py:54
  372.6 4.1 dynamic-slice_convert_fusion
  376.8 6.0 copy.28
  382.8 12.3 %reshape.56 = f32[12,32,96,32]{3,2,1,0:T(8,128)} reshape(f32[384,3072]{1,0:T(8,128)} %copy.28) | data formatting | bytes 9437184 | tf_op jit(solution)/shard_map/convert_element_type | solution.py:58
  395.1 22.5 %copy.29 = f32[12,32,96,32]{3,2,1,0:T(8,128)} copy(f32[12,32,96,32]{1,2,3,0:T(8,128)} %bitcast.72) | data formatting | bytes 9437184 | tf_op jit(solution)/shard_map/convert_element_type | solution.py:58
  417.6 14.6 %reshape.55 = f32[384,3072]{1,0:T(8,128)} reshape(f32[12,32,96,32]{3,2,1,0:T(8,128)} %copy.29) | data formatting | bytes 9437184 | tf_op jit(solution)/shard_map/convert_element_type | solution.py:58
  432.2 0.0 copy-start
  432.2 10.7 %convolution_convert_fusion = bf16[384,1536]{1,0:T(8,128)(2,1)} fusion(bf16[3072,1536]{1,0:T(8,128)(2,1)} %param.5, f32[384,3072]{1,0:T(8,128)} %reshape.55, bf16[2,384,3072]{2,1,0:T(8,128)(2,1)} %param.6), kind=kOutput, calls=%fused_computation.12 | convolution fusion | flops 3628007424 | bytes 17694720 | tf_op jit(solution)/shard_map/dot_general | solution.py:46
  442.8 0.0 all-gather.10.cloned.1.call-update
  442.8 0.0 copy-done
  442.9 0.7 copy.35
  443.6 185.0 %all-gather.10.cloned.1.call-done = bf16[3072,1536]{1,0:T(8,128)(2,1)} async-done(((bf16[384,1536]{1,0:T(8,128)(2,1)}), bf16[3072,1536]{1,0:T(8,128)(2,1)}) %all-gather.10.cloned.1.call-update) | async-done | bytes 9437200 | tf_op jit(solution)/shard_map/all_gather | solution.py:10
  628.6 5.7 reduce_sum.25
  634.3 1.4 copy.30
  635.7 6.8 %fusion.5 = bf16[1,384,1536]{1,2,0:T(8,128)(2,1)S(1)} fusion(bf16[1,384,1536]{1,2,0:T(8,128)(2,1)S(1)} %copy.35, bf16[384,1536]{0,1:T(8,128)(2,1)} %copy.30, f32[2,384,384]{2,1,0:T(8,128)} %param.8), kind=kOutput, calls=%fused_computation.14 | convolution fusion | flops 2723807232 | bytes 6488064 | tf_op jit(solution)/shard_map/dot_general | solution.py:22
  642.6 0.3 pad_maximum_fusion
  642.9 2.6 copy.31
Async XLA Ops:
  6.5 200.1 %all-gather.8.cloned.1.call-start = ((), (), s32[]{:S(2)}) async-start(), calls=%async_computation.1 | async-start | bytes 10616832 | tf_op jit(solution)/shard_map/all_gather | solution.py:10
  6.5 9.4 %copy-start.1 = (bf16[2,384,1536]{2,1,0:T(8,128)(2,1)S(1)}, bf16[2,384,1536]{2,1,0:T(8,128)(2,1)}, u32[]{:S(2)}) copy-start(bf16[2,384,1536]{2,1,0:T(8,128)(2,1)} %param.7) | copy-start | bytes 7077892
  15.9 356.7 %all-gather.6.cloned.1.call-start = ((), (), s32[]{:S(2)}) async-start(), calls=%async_computation | async-start | bytes 20054016 | tf_op jit(solution)/shard_map/all_gather | solution.py:54
  17.2 0.7 copy-start.2
  249.5 379.1 %all-gather.10.cloned.1.call-start = ((), (), s32[]{:S(2)}) async-start(), calls=%async_computation.2 | async-start | bytes 10616832 | tf_op jit(solution)/shard_map/all_gather | solution.py:10
  432.2 10.7 %copy-start = (bf16[1,384,1536]{2,1,0:T(8,128)(2,1)S(1)}, bf16[1,384,1536]{2,1,0:T(8,128)(2,1)}, u32[]{:S(2)}) copy-start(bf16[1,384,1536]{2,1,0:T(8,128)(2,1)} %get-tuple-element.6) | copy-start | bytes 3538948
Sparse Core Ops, SparseCore 0:
  16.0 190.5 all-gather.7
  249.6 122.9 all-gather.5
  443.0 185.5 all-gather.9
